TPU v7x, 128 devices: a whole 4x4x4 slice. The times are simulated.
128 devices in a mesh: seq: 8 (over z, core), exp: 16 (over y, x).
Axes of the slice: x: 4, y: 4, z: 4, core: 2. Of those that a mesh axis runs over, the one named last changes fastest.
Arguments:
- attn_query: bfloat16 [2048, 6144], P('seq', 'exp'), may hold values from -6 to 6
- attn_key: bfloat16 [2048, 6144], P('seq', 'exp'), may hold values from -6 to 6
- attn_value: bfloat16 [2048, 6144], P('seq', 'exp'), may hold values from -40 to 40
- log_decay: float32 [48, 2048], P('exp', 'seq'), may hold values from -1.5 to 0
- residual: bfloat16 [2048, 6144], P('seq', 'exp'), may hold values from -6 to 6
- norm_gain: bfloat16 [6144], P('exp'), may hold values from 0.099609375 to 1.8984375
- expert_ids: int32 [2048, 2], P('seq'), may hold values from 0 to 15, as said below
- router_weight: bfloat16 [6144, 16], P(None, 'seq'), may hold values from -0.078125 to 0.078125
- gate_weight: bfloat16 [16, 6144, 4608], P('seq', None, 'exp'), may hold values from -0.078125 to 0.078125
- up_weight: bfloat16 [16, 6144, 4608], P('seq', None, 'exp'), may hold values from -0.078125 to 0.078125
- down_weight: bfloat16 [16, 4608, 6144], P('seq', 'exp'), may hold values from -0.125 to 0.125
Outputs:
- layer_out: bfloat16 [2048, 6144], P('seq', 'exp')
Inputs may be any that keep to these rules, and one draw needn't show every extreme that they name: `expert_ids`: each row names two different experts. In every section of 256 consecutive rows no expert is named more than 64 times, and in every section some experts are named exactly 64 times.
All inputs are finite; a program needn't handle non-finite values.
Results may differ from a plain program's by a relative error of at most 0.017.
Values may be sent and summed in bfloat16 or wider, within the bound.
A program may use at most 192 MiB of HBM per device.

v0:
```python
import jax
import jax.numpy as jnp
from jax import lax
from jax.sharding import PartitionSpec as P


def shifted(array, axis, by):
    count = lax.axis_size(axis)
    pairs = [(i, i + by) for i in range(count) if 0 <= i + by < count]
    return lax.ppermute(array, axis, pairs)


def on_device(
    attn_query,
    attn_key,
    attn_value,
    log_decay,
    residual,
    norm_gain,
    expert_ids,
    router_weight,
    gate_weight,
    up_weight,
    down_weight,
):
    heads_here = log_decay.shape[0]
    length = log_decay.shape[1]
    head_size = attn_query.shape[1] // heads_here
    query_rows = attn_query.reshape(length, heads_here, head_size)
    key_rows = attn_key.reshape(length, heads_here, head_size)
    value_rows = attn_value.reshape(length, heads_here, head_size)
    cumulative = jnp.cumsum(log_decay, axis=1)
    causal = lax.broadcasted_iota(jnp.int32, (length, length), 0) >= lax.broadcasted_iota(
        jnp.int32, (length, length), 1
    )
    decay_gap = jnp.where(causal[None], cumulative[:, :, None] - cumulative[:, None, :], 0.0)
    decay_mask = jnp.where(causal[None], jnp.exp(decay_gap), 0.0)
    scores = jnp.einsum("thd,shd->hts", query_rows, key_rows, preferred_element_type=jnp.float32)
    weights = (scores * decay_mask).astype(jnp.bfloat16)
    intra_part = jnp.einsum("hts,shd->thd", weights, value_rows, preferred_element_type=jnp.float32)
    key_fade = jnp.exp(cumulative[:, -1:] - cumulative)
    scaled = (key_fade.T[:, :, None] * key_rows.astype(jnp.float32)).astype(jnp.bfloat16)
    local_state = jnp.einsum("shd,she->hde", scaled, value_rows, preferred_element_type=jnp.float32)
    section_fade = jnp.exp(cumulative[:, -1])
    incoming = jnp.zeros_like(local_state)
    for repeat_index in range(lax.axis_size("seq") - 1):
        incoming = shifted(section_fade[:, None, None] * incoming + local_state, "seq", 1)
    inter_part = jnp.einsum(
        "thd,hde->the", query_rows.astype(jnp.float32), incoming, precision=lax.Precision.HIGHEST
    )
    attn_out = intra_part + jnp.exp(cumulative).T[:, :, None] * inter_part
    mean_square = jnp.mean(attn_out * attn_out, axis=2, keepdims=True)
    normed = (attn_out / jnp.sqrt(mean_square + 1e-06)).reshape(length, heads_here * head_size)
    stream = (residual.astype(jnp.float32) + norm_gain.astype(jnp.float32) * normed).astype(
        jnp.bfloat16
    )
    experts_here = router_weight.shape[1]
    groups = lax.axis_size("seq")
    expert_count = experts_here * groups
    capacity = 4 * length // expert_count
    features = stream.shape[1]
    choices_per_token = expert_ids.shape[1]
    flat_ids = expert_ids.reshape(-1)
    expert_iota = lax.broadcasted_iota(jnp.int32, (1, expert_count), 1)
    onehot = (flat_ids[:, None] == expert_iota).astype(jnp.int32)
    running = jnp.cumsum(onehot, axis=0)
    slot_index = jnp.sum(running * onehot, axis=1) - 1
    target = flat_ids * capacity + slot_index
    place_iota = lax.broadcasted_iota(jnp.int32, (expert_count * capacity, 1), 0)
    route_matrix = (
        (place_iota == target[None, :])
        .astype(jnp.bfloat16)
        .reshape(expert_count * capacity, length, choices_per_token)
        .sum(axis=2)
    )
    outgoing = jnp.dot(route_matrix, stream, preferred_element_type=jnp.float32).astype(
        jnp.bfloat16
    )
    outgoing = outgoing.reshape(groups, experts_here, capacity, features)
    portion = lax.all_gather(
        lax.all_to_all(outgoing, "seq", split_axis=0, concat_axis=0, tiled=True),
        "exp",
        axis=3,
        tiled=True,
    )
    gate_acc = jnp.einsum(
        "sjcd,jdf->sjcf", portion, gate_weight, preferred_element_type=jnp.float32
    )
    upward = jnp.einsum("sjcd,jdf->sjcf", portion, up_weight, preferred_element_type=jnp.float32)
    logits = jnp.einsum("sjcd,dj->sjc", portion, router_weight, preferred_element_type=jnp.float32)
    hidden_act = (jax.nn.silu(gate_acc) * upward).astype(jnp.bfloat16)
    expert_out = lax.psum_scatter(
        jnp.einsum(
            "sjcf,jfd->dsjc", hidden_act, down_weight, preferred_element_type=jnp.float32
        ).astype(jnp.bfloat16),
        "exp",
        scatter_dimension=0,
        tiled=True,
    ).astype(jnp.float32)
    routed = (jax.nn.sigmoid(logits)[None] * expert_out).astype(jnp.bfloat16)
    returned = lax.all_to_all(routed, "seq", split_axis=1, concat_axis=1, tiled=True)
    returned = returned.reshape(features, expert_count * capacity)
    combined = lax.dot_general(
        route_matrix, returned, (((0,), (1,)), ((), ())), preferred_element_type=jnp.float32
    )
    return (stream.astype(jnp.float32) + combined).astype(jnp.bfloat16)


def solution(mesh):
    in_specs = (
        P("seq", "exp"),
        P("seq", "exp"),
        P("seq", "exp"),
        P("exp", "seq"),
        P("seq", "exp"),
        P("exp"),
        P("seq", None),
        P(None, "seq"),
        P("seq", None, "exp"),
        P("seq", None, "exp"),
        P("seq", "exp", None),
    )
    out_specs = P("seq", "exp")
    return jax.shard_map(
        on_device, mesh=mesh, in_specs=in_specs, out_specs=out_specs, check_vma=False
    )
```

profile of v0, /device:TPU:1, one launch (start us, length us, event | category | flops | bytes accessed | tf_op | source)
XLA Modules:
  0.0 400.8 jit_solution(6427846024970069958)
XLA Ops:
  7.3 0.9 reduce-window.14
  8.8 1.1 copy.80
  9.9 1.1 copy.85
  11.2 4.9 %collective-permute-start = (f32[3,128,128]{2,1,0:T(8,128)S(1)}, f32[3,128,128]{2,1,0:T(8,128)S(1)}, u32[]{:S(2)}, u32[]{:S(2)}) collective-permute-start(f32[3,128,128]{2,1,0:T(8,128)S(1)} %get-tuple-element.9), channel_id=1, source_target_pairs={{0,16},{16,32},{32,48},{48,64},{64,80},{80,96},{96,112},{1,17},{17... | collective-permute-start | bytes 589832 | tf_op jit(solution)/shard_map/ppermute | solution.py:10
  18.8 4.4 %collective-permute-start.1 = (f32[3,128,128]{2,1,0:T(8,128)S(1)}, f32[3,128,128]{2,1,0:T(8,128)S(1)}, u32[]{:S(2)}, u32[]{:S(2)}) collective-permute-start(f32[3,128,128]{2,1,0:T(8,128)S(1)} %multiply_add_fusion.5), channel_id=1, source_target_pairs={{0,16},{16,32},{32,48},{48,64},{64,80},{80,96},{96,112},{1,17},{17... | collective-permute-start | bytes 589832 | tf_op jit(solution)/shard_map/ppermute | solution.py:10
  23.2 1.2 reduce-window.16
  24.4 1.4 collective-permute-done.1
  25.9 4.4 %collective-permute-start.2 = (f32[3,128,128]{2,1,0:T(8,128)S(1)}, f32[3,128,128]{2,1,0:T(8,128)S(1)}, u32[]{:S(2)}, u32[]{:S(2)}) collective-permute-start(f32[3,128,128]{2,1,0:T(8,128)S(1)} %multiply_add_fusion.4), channel_id=1, source_target_pairs={{0,16},{16,32},{32,48},{48,64},{64,80},{80,96},{96,112},{1,17},{17... | collective-permute-start | bytes 589832 | tf_op jit(solution)/shard_map/ppermute | solution.py:10
  30.7 2.2 collective-permute-done.2
  33.0 4.4 %collective-permute-start.3 = (f32[3,128,128]{2,1,0:T(8,128)S(1)}, f32[3,128,128]{2,1,0:T(8,128)S(1)}, u32[]{:S(2)}, u32[]{:S(2)}) collective-permute-start(f32[3,128,128]{2,1,0:T(8,128)S(1)} %multiply_add_fusion.3), channel_id=1, source_target_pairs={{0,16},{16,32},{32,48},{48,64},{64,80},{80,96},{96,112},{1,17},{17... | collective-permute-start | bytes 589832 | tf_op jit(solution)/shard_map/ppermute | solution.py:10
  37.6 1.1 copy.79
  38.7 1.3 collective-permute-done.3
  40.1 4.4 %collective-permute-start.4 = (f32[3,128,128]{2,1,0:T(8,128)S(1)}, f32[3,128,128]{2,1,0:T(8,128)S(1)}, u32[]{:S(2)}, u32[]{:S(2)}) collective-permute-start(f32[3,128,128]{2,1,0:T(8,128)S(1)} %multiply_add_fusion.2), channel_id=1, source_target_pairs={{0,16},{16,32},{32,48},{48,64},{64,80},{80,96},{96,112},{1,17},{17... | collective-permute-start | bytes 589832 | tf_op jit(solution)/shard_map/ppermute | solution.py:10
  45.2 1.9 collective-permute-done.4
  47.1 4.4 %collective-permute-start.5 = (f32[3,128,128]{2,1,0:T(8,128)S(1)}, f32[3,128,128]{2,1,0:T(8,128)S(1)}, u32[]{:S(2)}, u32[]{:S(2)}) collective-permute-start(f32[3,128,128]{2,1,0:T(8,128)S(1)} %multiply_add_fusion.1), channel_id=1, source_target_pairs={{0,16},{16,32},{32,48},{48,64},{64,80},{80,96},{96,112},{1,17},{17... | collective-permute-start | bytes 589832 | tf_op jit(solution)/shard_map/ppermute | solution.py:10
  52.0 2.1 collective-permute-done.5
  54.2 4.4 %collective-permute-start.6 = (f32[3,128,128]{2,1,0:T(8,128)S(1)}, f32[3,128,128]{2,1,0:T(8,128)S(1)}, u32[]{:S(2)}, u32[]{:S(2)}) collective-permute-start(f32[3,128,128]{2,1,0:T(8,128)S(1)} %multiply_add_fusion), channel_id=1, source_target_pairs={{0,16},{16,32},{32,48},{48,64},{64,80},{80,96},{96,112},{1,17},{17... | collective-permute-start | bytes 589832 | tf_op jit(solution)/shard_map/ppermute | solution.py:10
  59.1 2.1 collective-permute-done.6
  62.4 18.3 %all_to_all.10 = bf16[8,2,64,384]{3,2,1,0:T(8,128)(2,1)S(1)} all-to-all(bf16[8,2,64,384]{3,2,1,0:T(8,128)(2,1)S(1)} %bitcast.110), channel_id=1, replica_groups=mesh['seq'=8,'exp'=16] {'seq'}, dimensions={0} | all-to-all | bytes 1572864 | tf_op jit(solution)/shard_map/all_to_all | solution.py:81
  80.6 1.0 copy.95
  81.9 98.5 %all-gather.2.cloned.1.call-done = bf16[8,2,64,6144]{3,2,0,1:T(8,128)(2,1)} async-done(((bf16[8,2,64,384]{3,2,0,1:T(8,128)(2,1)}), bf16[8,2,64,6144]{3,2,0,1:T(8,128)(2,1)}) %all-gather.2.cloned.1.call-update) | async-done | bytes 12582928 | tf_op jit(solution)/shard_map/all_gather | solution.py:80
  180.3 11.8 %fusion.3 = f32[2,8,64,288]{3,2,1,0:T(8,128)S(1)} fusion(bf16[8,2,64,6144]{3,2,0,1:T(8,128)(2,1)} %all-gather.2.cloned.1.call-done, bf16[2,6144,288]{1,2,0:T(8,128)(2,1)} %param.19), kind=kOutput, calls=%fused_computation.4 | convolution fusion | flops 3623878656 | bytes 20840448 | tf_op jit(solution)/shard_map/sjcd,jdf->sjcf/dot_general | solution.py:86
  192.1 8.9 %fusion.6 = bf16[8,2,64,288]{3,2,0,1:T(8,128)(2,1)S(1)} fusion(f32[2,8,64,288]{3,2,1,0:T(8,128)S(1)} %fusion.3, bf16[8,2,64,6144]{3,2,0,1:T(8,128)(2,1)S(1)} %copy-done.1, bf16[2,6144,288]{1,2,0:T(8,128)(2,1)} %param.20), kind=kOutput, calls=%fused_computation.9 | convolution fusion | flops 3625648128 | bytes 21430272 | tf_op jit(solution)/shard_map/sjcd,jdf->sjcf/dot_general | solution.py:89
  201.1 12.6 %convert_bitcast_fusion = bf16[6144,8,2,64]{0,3,1,2:T(8,128)(2,1)} fusion(bf16[8,2,64,288]{3,2,0,1:T(8,128)(2,1)S(1)} %fusion.6, bf16[2,288,6144]{2,1,0:T(8,128)(2,1)} %param.21), kind=kOutput, calls=%fused_computation | convolution fusion | flops 3630170112 | bytes 20250624 | tf_op jit(solution)/shard_map/sjcf,jfd->dsjc/dot_general | solution.py:93
  213.7 29.7 %copy.107 = bf16[6144,8,2,64]{3,1,2,0:T(8,128)(2,1)} copy(bf16[6144,8,2,64]{0,3,1,2:T(8,128)(2,1)} %convert_bitcast_fusion) | data formatting | bytes 25165824
  243.4 33.4 %reshape.128 = bf16[6144,1024]{1,0:T(8,128)(2,1)} reshape(bf16[6144,2,8,64]{3,2,1,0:T(8,128)(2,1)} %bitcast.108) | data formatting | bytes 25165824
  276.8 7.9 %fusion.29 = f32[2,1,8,64]{3,1,2,0:T(1,128)S(1)} fusion(bf16[8,2,64,6144]{3,2,0,1:T(8,128)(2,1)} %all-gather.2.cloned.1.call-done, bf16[6144,2,1,1]{0,1,2,3:T(2,128)(2,1)S(1)} %bitcast.107), kind=kOutput, calls=%fused_computation.49 | convolution fusion | flops 12582912 | bytes 12611584 | tf_op jit(solution)/shard_map/sjcd,dj->sjc/dot_general | solution.py:90
  284.7 86.8 %reduce-scatter.4.cloned.1.call-done = bf16[384,1024]{1,0:T(8,128)(2,1)} async-done(((bf16[6144,1024]{1,0:T(8,128)(2,1)}), bf16[384,1024]{1,0:T(8,128)(2,1)}) %reduce-scatter.4.cloned.1.call-update) | async-done | bytes 786448
  371.5 2.5 reshape.129
  374.0 1.2 copy.108
  375.5 17.3 %all_to_all.11 = bf16[384,8,2,64]{0,3,2,1:T(8,128)(2,1)S(1)} all-to-all(bf16[384,8,2,64]{0,3,2,1:T(8,128)(2,1)S(1)} %copy.96), channel_id=1, replica_groups=mesh['seq'=8,'exp'=16] {'seq'}, dimensions={1} | all-to-all | bytes 1572864 | tf_op jit(solution)/shard_map/all_to_all | solution.py:101
  392.8 1.1 fusion.17
  (55 shorter events, 8.6 us)
Async XLA Ops:
  6.5 270.3 %copy-start = (bf16[6144,2]{0,1:T(2,128)(2,1)S(1)}, bf16[6144,2]{0,1:T(2,128)(2,1)}, u32[]{:S(2)}) copy-start(bf16[6144,2]{0,1:T(2,128)(2,1)} %param.18) | copy-start | bytes 73732
  6.5 55.3 %copy-start.2 = (bf16[256,384]{1,0:T(8,128)(2,1)S(1)}, bf16[256,384]{1,0:T(8,128)(2,1)}, u32[]{:S(2)}) copy-start(bf16[256,384]{1,0:T(8,128)(2,1)} %param.15) | copy-start | bytes 589828
  6.5 173.8 %all-gather.2.cloned.1.call-start = ((), (), s32[]{:S(2)}) async-start(), calls=%async_computation.3 | async-start | bytes 13369344 | tf_op jit(solution)/shard_map/all_gather | solution.py:80
  11.2 7.5 %collective-permute-start = (f32[3,128,128]{2,1,0:T(8,128)S(1)}, f32[3,128,128]{2,1,0:T(8,128)S(1)}, u32[]{:S(2)}, u32[]{:S(2)}) collective-permute-start(f32[3,128,128]{2,1,0:T(8,128)S(1)} %get-tuple-element.9), channel_id=1, source_target_pairs={{0,16},{16,32},{32,48},{48,64},{64,80},{80,96},{96,112},{1,17},{17... | collective-permute-start | bytes 589832 | tf_op jit(solution)/shard_map/ppermute | solution.py:10
  18.8 7.0 %collective-permute-start.1 = (f32[3,128,128]{2,1,0:T(8,128)S(1)}, f32[3,128,128]{2,1,0:T(8,128)S(1)}, u32[]{:S(2)}, u32[]{:S(2)}) collective-permute-start(f32[3,128,128]{2,1,0:T(8,128)S(1)} %multiply_add_fusion.5), channel_id=1, source_target_pairs={{0,16},{16,32},{32,48},{48,64},{64,80},{80,96},{96,112},{1,17},{17... | collective-permute-start | bytes 589832 | tf_op jit(solution)/shard_map/ppermute | solution.py:10
  25.9 7.0 %collective-permute-start.2 = (f32[3,128,128]{2,1,0:T(8,128)S(1)}, f32[3,128,128]{2,1,0:T(8,128)S(1)}, u32[]{:S(2)}, u32[]{:S(2)}) collective-permute-start(f32[3,128,128]{2,1,0:T(8,128)S(1)} %multiply_add_fusion.4), channel_id=1, source_target_pairs={{0,16},{16,32},{32,48},{48,64},{64,80},{80,96},{96,112},{1,17},{17... | collective-permute-start | bytes 589832 | tf_op jit(solution)/shard_map/ppermute | solution.py:10
  33.0 7.0 %collective-permute-start.3 = (f32[3,128,128]{2,1,0:T(8,128)S(1)}, f32[3,128,128]{2,1,0:T(8,128)S(1)}, u32[]{:S(2)}, u32[]{:S(2)}) collective-permute-start(f32[3,128,128]{2,1,0:T(8,128)S(1)} %multiply_add_fusion.3), channel_id=1, source_target_pairs={{0,16},{16,32},{32,48},{48,64},{64,80},{80,96},{96,112},{1,17},{17... | collective-permute-start | bytes 589832 | tf_op jit(solution)/shard_map/ppermute | solution.py:10
  40.1 7.0 %collective-permute-start.4 = (f32[3,128,128]{2,1,0:T(8,128)S(1)}, f32[3,128,128]{2,1,0:T(8,128)S(1)}, u32[]{:S(2)}, u32[]{:S(2)}) collective-permute-start(f32[3,128,128]{2,1,0:T(8,128)S(1)} %multiply_add_fusion.2), channel_id=1, source_target_pairs={{0,16},{16,32},{32,48},{48,64},{64,80},{80,96},{96,112},{1,17},{17... | collective-permute-start | bytes 589832 | tf_op jit(solution)/shard_map/ppermute | solution.py:10
  47.1 7.0 %collective-permute-start.5 = (f32[3,128,128]{2,1,0:T(8,128)S(1)}, f32[3,128,128]{2,1,0:T(8,128)S(1)}, u32[]{:S(2)}, u32[]{:S(2)}) collective-permute-start(f32[3,128,128]{2,1,0:T(8,128)S(1)} %multiply_add_fusion.1), channel_id=1, source_target_pairs={{0,16},{16,32},{32,48},{48,64},{64,80},{80,96},{96,112},{1,17},{17... | collective-permute-start | bytes 589832 | tf_op jit(solution)/shard_map/ppermute | solution.py:10
  54.2 7.0 %collective-permute-start.6 = (f32[3,128,128]{2,1,0:T(8,128)S(1)}, f32[3,128,128]{2,1,0:T(8,128)S(1)}, u32[]{:S(2)}, u32[]{:S(2)}) collective-permute-start(f32[3,128,128]{2,1,0:T(8,128)S(1)} %multiply_add_fusion), channel_id=1, source_target_pairs={{0,16},{16,32},{32,48},{48,64},{64,80},{80,96},{96,112},{1,17},{17... | collective-permute-start | bytes 589832 | tf_op jit(solution)/shard_map/ppermute | solution.py:10
  81.6 289.9 %reduce-scatter.4.cloned.1.call-start = ((), (), s32[]{:S(2)}) async-start(), calls=%async_computation.4 | async-start | bytes 13369344
  180.3 11.8 %copy-start.1 = (bf16[8,2,64,6144]{3,2,0,1:T(8,128)(2,1)S(1)}, bf16[8,2,64,6144]{3,2,0,1:T(8,128)(2,1)}, u32[]{:S(2)}) copy-start(bf16[8,2,64,6144]{3,2,0,1:T(8,128)(2,1)} %all-gather.2.cloned.1.call-done) | copy-start | bytes 37748740
Sparse Core Ops, SparseCore 0:
  81.7 98.5 all-gather.1
  276.9 94.5 reduce-scatter.3
where the time goes:
time: 403 us; the launch traced here: 401 us
  waiting for transfers between devices  197 us (49%)
  local copies, waits for them, and re-layouts  73.9 us (18%)
  matrix products  43.9 us (11%)
  blocking collectives  35.6 us (9%)
  starting transfers between devices  31.5 us (8%)
  between operations  13.7 us (3%)
  other arithmetic  5.1 us (1%)
    all_gather x1, waiting for transfers between devices, on_device(): lax.all_gather(lax.all_to_all(outgoing, 'seq', split_axis=0, concat_axis=...  98.5 us
    unnamed x3, waiting for transfers between devices  86.8 us
    unnamed x16, local copies, waits for them, and re-layouts  70.9 us
    ppermute x7, starting transfers between devices, shifted(): return lax.ppermute(array, axis, pairs)  31.3 us
    all_to_all x1, blocking collectives, on_device(): lax.all_to_all(outgoing, 'seq', split_axis=0, concat_axis=0, tiled=True)  18.3 us
    all_to_all x1, blocking collectives, on_device(): lax.all_to_all(routed, 'seq', split_axis=1, concat_axis=1, tiled=True)  17.3 us
    dot_general x1, matrix products, on_device(): jnp.einsum('sjcf,jfd->dsjc', hidden_act, down_weight, preferred_element_t...  12.6 us
    dot_general x1, matrix products, on_device(): jnp.einsum('sjcd,jdf->sjcf', portion, gate_weight, preferred_element_type...  11.8 us
  transfers between devices with their start and end apart: 9, of which 9 were waited for; matrix products, arithmetic and copies ran while one was open for 4% of the time, Pallas kernels for 0%

commit v1 on v0

--- a/solution.py
+++ b/solution.py
@@ -77,11 +77,17 @@
         jnp.bfloat16
     )
     outgoing = outgoing.reshape(groups, experts_here, capacity, features)
-    portion = lax.all_gather(
-        lax.all_to_all(outgoing, "seq", split_axis=0, concat_axis=0, tiled=True),
-        "exp",
+    portion = jnp.concatenate(
+        lax.all_to_all(
+            jnp.stack(
+                [lax.all_to_all(outgoing, "seq", split_axis=0, concat_axis=0, tiled=True)]
+                * lax.axis_size("exp")
+            ),
+            "exp",
+            0,
+            0,
+        ),
         axis=3,
-        tiled=True,
     )
     gate_acc = jnp.einsum(
         "sjcd,jdf->sjcf", portion, gate_weight, preferred_element_type=jnp.float32

time: 403 us -> 456 us (1.13)
  blocking collectives: 35.6 us -> 182 us
  waiting for transfers between devices: 197 us -> 95.4 us
  local copies, waits for them, and re-layouts: 73.9 us -> 83 us
    all_to_all x0 -> x1, blocking collectives: none -> 146 us  [on_device(): lax.all_to_all(jnp.stack([lax.all_to_all(outgoing, 'seq', split_axis=0, c...]
    all_gather x1 -> x0, waiting for transfers between devices: 98.5 us -> none  [on_device(): lax.all_gather(lax.all_to_all(outgoing, 'seq', split_axis=0, concat_axis=...]
    another operation x4 -> x5, local copies, waits for them, and re-layouts: 0.32 us -> 7.02 us  [the longest x1 6.7 us: on_device(): jnp.stack([lax.all_to_all(outgoing, 'seq', split_axis=0, concat_axis=0, t...]
    unnamed x3 -> x2, waiting for transfers between devices: 86.8 us -> 83.6 us
  transfers between devices with their start and end apart: 9 -> 8, of which waited for: 9 -> 8; matrix products, arithmetic and copies ran while one was open for 4% -> 3% of each run, Pallas kernels for 0% -> 0%
where the time goes in v1:
time: 456 us; the launch traced here: 454 us
  blocking collectives  182 us (40%)
  waiting for transfers between devices  95.4 us (21%)
  local copies, waits for them, and re-layouts  83 us (18%)
  matrix products  43.6 us (10%)
  starting transfers between devices  31.3 us (7%)
  between operations  13.7 us (3%)
  other arithmetic  5.1 us (1%)
    all_to_all x1, blocking collectives, on_device(): lax.all_to_all(jnp.stack([lax.all_to_all(outgoing, 'seq', split_axis=0, c...  146 us
    unnamed x2, waiting for transfers between devices  83.6 us
    unnamed x16, local copies, waits for them, and re-layouts  70.9 us
    ppermute x7, starting transfers between devices, shifted(): return lax.ppermute(array, axis, pairs)  31.3 us
    all_to_all x1, blocking collectives, on_device(): lax.all_to_all(outgoing, 'seq', split_axis=0, concat_axis=0, tiled=True)  18.3 us
    all_to_all x1, blocking collectives, on_device(): lax.all_to_all(routed, 'seq', split_axis=1, concat_axis=1, tiled=True)  17.3 us
    dot_general x1, matrix products, on_device(): jnp.einsum('sjcf,jfd->dsjc', hidden_act, down_weight, preferred_element_t...  12.6 us
    ppermute x7, waiting for transfers between devices, shifted(): return lax.ppermute(array, axis, pairs)  11.8 us
  transfers between devices with their start and end apart: 8, of which 8 were waited for; matrix products, arithmetic and copies ran while one was open for 3% of the time, Pallas kernels for 0%

profile of v1, /device:TPU:1, one launch (start us, length us, event | category | flops | bytes accessed | tf_op | source)
XLA Modules:
  0.0 453.9 jit_solution(14732031231389235297)
XLA Ops:
  8.8 1.1 copy.82
  9.9 1.1 copy.87
  11.2 4.9 %collective-permute-start = (f32[3,128,128]{2,1,0:T(8,128)S(1)}, f32[3,128,128]{2,1,0:T(8,128)S(1)}, u32[]{:S(2)}, u32[]{:S(2)}) collective-permute-start(f32[3,128,128]{2,1,0:T(8,128)S(1)} %get-tuple-element.9), channel_id=1, source_target_pairs={{0,16},{16,32},{32,48},{48,64},{64,80},{80,96},{96,112},{1,17},{17... | collective-permute-start | bytes 589832 | tf_op jit(solution)/shard_map/ppermute | solution.py:10
  18.8 4.4 collective-permute-start.1
  23.2 1.2 reduce-window.16
  24.4 1.4 collective-permute-done.1
  25.9 4.4 collective-permute-start.2
  30.7 2.2 collective-permute-done.2
  33.0 4.4 collective-permute-start.3
  37.6 1.1 copy.81
  38.7 1.3 collective-permute-done.3
  40.1 4.4 collective-permute-start.4
  45.2 1.9 collective-permute-done.4
  47.1 4.4 collective-permute-start.5
  52.0 2.1 collective-permute-done.5
  54.2 4.4 collective-permute-start.6
  59.1 2.1 collective-permute-done.6
  62.4 18.3 %all_to_all.15 = bf16[8,2,64,384]{3,2,1,0:T(8,128)(2,1)S(1)} all-to-all(bf16[8,2,64,384]{3,2,1,0:T(8,128)(2,1)S(1)} %bitcast.117), channel_id=1, replica_groups=mesh['seq'=8,'exp'=16] {'seq'}, dimensions={0} | all-to-all | bytes 1572864 | tf_op jit(solution)/shard_map/all_to_all | solution.py:83
  80.7 6.7 %stack.2 = bf16[16,8,2,64,384]{4,3,1,2,0:T(8,128)(2,1)} broadcast(bf16[8,2,64,384]{3,2,0,1:T(8,128)(2,1)S(1)} %copy.97), dimensions={1,2,3,4} | broadcast | bytes 13369344 | tf_op jit(solution)/shard_map/stack | solution.py:82
  87.4 146.2 %all_to_all.16 = bf16[16,8,2,64,384]{4,3,1,2,0:T(8,128)(2,1)S(1)} all-to-all(bf16[16,8,2,64,384]{4,3,1,2,0:T(8,128)(2,1)} %stack.2), channel_id=1, replica_groups=mesh['seq'=8,'exp'=16] {'exp'}, dimensions={0} | all-to-all | bytes 25165824 | tf_op jit(solution)/shard_map/all_to_all | solution.py:81
  233.7 3.2 copy.114
  236.9 11.6 %fusion.3 = f32[2,8,64,288]{3,2,1,0:T(8,128)S(1)} fusion(bf16[8,2,64,6144]{3,2,0,1:T(8,128)(2,1)S(1)} %bitcast.112, bf16[2,6144,288]{1,2,0:T(8,128)(2,1)} %param.19), kind=kOutput, calls=%fused_computation.4 | convolution fusion | flops 3623878656 | bytes 20840448 | tf_op jit(solution)/shard_map/sjcd,jdf->sjcf/dot_general | solution.py:92
  248.5 8.9 %fusion.6 = bf16[8,2,64,288]{3,2,0,1:T(8,128)(2,1)S(1)} fusion(f32[2,8,64,288]{3,2,1,0:T(8,128)S(1)} %fusion.3, bf16[8,2,64,6144]{3,2,0,1:T(8,128)(2,1)S(1)} %bitcast.113, bf16[2,6144,288]{1,2,0:T(8,128)(2,1)} %param.20), kind=kOutput, calls=%fused_computation.9 | convolution fusion | flops 3625648128 | bytes 21430272 | tf_op jit(solution)/shard_map/sjcd,jdf->sjcf/dot_general | solution.py:95
  257.4 12.6 %convert_bitcast_fusion = bf16[6144,8,2,64]{0,3,1,2:T(8,128)(2,1)} fusion(bf16[8,2,64,288]{3,2,0,1:T(8,128)(2,1)S(1)} %fusion.6, bf16[2,288,6144]{2,1,0:T(8,128)(2,1)} %param.21), kind=kOutput, calls=%fused_computation | convolution fusion | flops 3630170112 | bytes 20250624 | tf_op jit(solution)/shard_map/sjcf,jfd->dsjc/dot_general | solution.py:99
  270.0 29.7 %copy.110 = bf16[6144,8,2,64]{3,1,2,0:T(8,128)(2,1)} copy(bf16[6144,8,2,64]{0,3,1,2:T(8,128)(2,1)} %convert_bitcast_fusion) | data formatting | bytes 25165824
  299.7 33.4 %reshape.138 = bf16[6144,1024]{1,0:T(8,128)(2,1)} reshape(bf16[6144,2,8,64]{3,2,1,0:T(8,128)(2,1)} %bitcast.111) | data formatting | bytes 25165824
  333.1 7.9 %fusion.29 = f32[2,1,8,64]{3,1,2,0:T(1,128)S(1)} fusion(bf16[8,2,64,6144]{3,2,0,1:T(8,128)(2,1)} %bitcast.114, bf16[6144,2,1,1]{0,1,2,3:T(2,128)(2,1)S(1)} %bitcast.110), kind=kOutput, calls=%fused_computation.49 | convolution fusion | flops 12582912 | bytes 12611584 | tf_op jit(solution)/shard_map/sjcd,dj->sjc/dot_general | solution.py:96
  341.0 83.5 %reduce-scatter.4.cloned.1.call-done = bf16[384,1024]{1,0:T(8,128)(2,1)} async-done(((bf16[6144,1024]{1,0:T(8,128)(2,1)}), bf16[384,1024]{1,0:T(8,128)(2,1)}) %reduce-scatter.4.cloned.1.call-update) | async-done | bytes 786448
  424.6 2.5 reshape.139
  427.1 1.2 copy.111
  428.6 17.3 %all_to_all.17 = bf16[384,8,2,64]{0,3,2,1:T(8,128)(2,1)S(1)} all-to-all(bf16[384,8,2,64]{0,3,2,1:T(8,128)(2,1)S(1)} %copy.99), channel_id=1, replica_groups=mesh['seq'=8,'exp'=16] {'seq'}, dimensions={1} | all-to-all | bytes 1572864 | tf_op jit(solution)/shard_map/all_to_all | solution.py:107
  445.9 1.1 fusion.17
  (55 shorter events, 9.4 us)
Async XLA Ops:
  6.5 326.6 %copy-start = (bf16[6144,2]{0,1:T(2,128)(2,1)S(1)}, bf16[6144,2]{0,1:T(2,128)(2,1)}, u32[]{:S(2)}) copy-start(bf16[6144,2]{0,1:T(2,128)(2,1)} %param.18) | copy-start | bytes 73732
  6.5 55.3 %copy-start.2 = (bf16[256,384]{1,0:T(8,128)(2,1)S(1)}, bf16[256,384]{1,0:T(8,128)(2,1)}, u32[]{:S(2)}) copy-start(bf16[256,384]{1,0:T(8,128)(2,1)} %param.15) | copy-start | bytes 589828
  6.5 418.0 %reduce-scatter.4.cloned.1.call-start = ((), (), s32[]{:S(2)}) async-start(), calls=%async_computation.4 | async-start | bytes 13369344
  11.2 7.5 %collective-permute-start = (f32[3,128,128]{2,1,0:T(8,128)S(1)}, f32[3,128,128]{2,1,0:T(8,128)S(1)}, u32[]{:S(2)}, u32[]{:S(2)}) collective-permute-start(f32[3,128,128]{2,1,0:T(8,128)S(1)} %get-tuple-element.9), channel_id=1, source_target_pairs={{0,16},{16,32},{32,48},{48,64},{64,80},{80,96},{96,112},{1,17},{17... | collective-permute-start | bytes 589832 | tf_op jit(solution)/shard_map/ppermute | solution.py:10
  18.8 7.0 %collective-permute-start.1 = (f32[3,128,128]{2,1,0:T(8,128)S(1)}, f32[3,128,128]{2,1,0:T(8,128)S(1)}, u32[]{:S(2)}, u32[]{:S(2)}) collective-permute-start(f32[3,128,128]{2,1,0:T(8,128)S(1)} %multiply_add_fusion.5), channel_id=1, source_target_pairs={{0,16},{16,32},{32,48},{48,64},{64,80},{80,96},{96,112},{1,17},{17... | collective-permute-start | bytes 589832 | tf_op jit(solution)/shard_map/ppermute | solution.py:10
  25.9 7.0 %collective-permute-start.2 = (f32[3,128,128]{2,1,0:T(8,128)S(1)}, f32[3,128,128]{2,1,0:T(8,128)S(1)}, u32[]{:S(2)}, u32[]{:S(2)}) collective-permute-start(f32[3,128,128]{2,1,0:T(8,128)S(1)} %multiply_add_fusion.4), channel_id=1, source_target_pairs={{0,16},{16,32},{32,48},{48,64},{64,80},{80,96},{96,112},{1,17},{17... | collective-permute-start | bytes 589832 | tf_op jit(solution)/shard_map/ppermute | solution.py:10
  33.0 7.0 %collective-permute-start.3 = (f32[3,128,128]{2,1,0:T(8,128)S(1)}, f32[3,128,128]{2,1,0:T(8,128)S(1)}, u32[]{:S(2)}, u32[]{:S(2)}) collective-permute-start(f32[3,128,128]{2,1,0:T(8,128)S(1)} %multiply_add_fusion.3), channel_id=1, source_target_pairs={{0,16},{16,32},{32,48},{48,64},{64,80},{80,96},{96,112},{1,17},{17... | collective-permute-start | bytes 589832 | tf_op jit(solution)/shard_map/ppermute | solution.py:10
  40.1 7.0 %collective-permute-start.4 = (f32[3,128,128]{2,1,0:T(8,128)S(1)}, f32[3,128,128]{2,1,0:T(8,128)S(1)}, u32[]{:S(2)}, u32[]{:S(2)}) collective-permute-start(f32[3,128,128]{2,1,0:T(8,128)S(1)} %multiply_add_fusion.2), channel_id=1, source_target_pairs={{0,16},{16,32},{32,48},{48,64},{64,80},{80,96},{96,112},{1,17},{17... | collective-permute-start | bytes 589832 | tf_op jit(solution)/shard_map/ppermute | solution.py:10
  47.1 7.0 %collective-permute-start.5 = (f32[3,128,128]{2,1,0:T(8,128)S(1)}, f32[3,128,128]{2,1,0:T(8,128)S(1)}, u32[]{:S(2)}, u32[]{:S(2)}) collective-permute-start(f32[3,128,128]{2,1,0:T(8,128)S(1)} %multiply_add_fusion.1), channel_id=1, source_target_pairs={{0,16},{16,32},{32,48},{48,64},{64,80},{80,96},{96,112},{1,17},{17... | collective-permute-start | bytes 589832 | tf_op jit(solution)/shard_map/ppermute | solution.py:10
  54.2 7.0 %collective-permute-start.6 = (f32[3,128,128]{2,1,0:T(8,128)S(1)}, f32[3,128,128]{2,1,0:T(8,128)S(1)}, u32[]{:S(2)}, u32[]{:S(2)}) collective-permute-start(f32[3,128,128]{2,1,0:T(8,128)S(1)} %multiply_add_fusion), channel_id=1, source_target_pairs={{0,16},{16,32},{32,48},{48,64},{64,80},{80,96},{96,112},{1,17},{17... | collective-permute-start | bytes 589832 | tf_op jit(solution)/shard_map/ppermute | solution.py:10
  236.9 11.6 %copy-start.1 = (bf16[16,2,8,8,8,384]{5,4,0,3,2,1:T(8,128)(2,1)}, bf16[16,2,8,8,8,384]{5,4,0,3,2,1:T(8,128)(2,1)S(1)}, u32[]{:S(2)}) copy-start(bf16[16,2,8,8,8,384]{5,4,0,3,2,1:T(8,128)(2,1)S(1)} %copy.114) | copy-start | bytes 37748740
Sparse Core Ops, SparseCore 0:
  333.2 91.2 reduce-scatter.3
